TPU v7x, 32 devices: a whole 2x2x4 slice. The times are simulated.
32 devices in a mesh: dp: 16 (over z, y, x), mp: 2 (over core).
Axes of the slice: x: 2, y: 2, z: 4, core: 2. Of those that a mesh axis runs over, the one named last changes fastest.
Arguments:
- value_grads: bfloat16 [16, 24, 128, 128], P('dp', 'mp'), may hold values from -2 to 2
- key_grads: bfloat16 [16, 2, 16, 128, 128], P('dp', 'mp'), may hold values from -0.75 to 0.75
- owners: int32 [40, 1], P('mp'), may hold values from 0 to 15; in each aligned block of 20 rows (0 to 19, 20 to 39, ...) at most 2 rows name the same one
- weights: float32 [16, 2, 2, 128, 128], P('dp', 'mp'), may hold values from -6 to 6
- left: float32 [16, 2, 2, 128, 128], P('dp', 'mp'), may hold values from -0.25 to 4, as said below
- right: float32 [16, 2, 2, 128, 128], P('dp', 'mp'), may hold values from -0.25 to 4, as said below
- left_root: float32 [16, 2, 2, 128, 128], P('dp', 'mp'), may hold values from -0.25 to 4
- right_root: float32 [16, 2, 2, 128, 128], P('dp', 'mp'), may hold values from -0.25 to 4
- second: float32 [16, 2, 2, 128, 128], P('dp', 'mp'), may hold values from 0.001 to 0.1
Outputs:
- new_weights: float32 [16, 2, 2, 128, 128], P('dp', 'mp')
- new_left: float32 [16, 2, 2, 128, 128], P('dp', 'mp')
- new_right: float32 [16, 2, 2, 128, 128], P('dp', 'mp')
- new_second: float32 [16, 2, 2, 128, 128], P('dp', 'mp')
- new_values: bfloat16 [24, 128, 128], P('mp')
- new_keys: bfloat16 [16, 128, 128], P('mp')
Inputs may be any that keep to these rules, and one draw needn't show every extreme that they name: `owners`: within each aligned block of 20 rows (one index of mp) no dp index appears more than 2 times; some appears exactly 2 times. `left`: Symmetric. `right`: Symmetric.
All inputs are finite; a program needn't handle non-finite values.
Results may differ from a plain program's by a relative error of at most 0.0035.
Values may be sent and summed in bfloat16 or wider, within the bound.
A program may use at most 64 MiB of HBM per device.

v0:
```python
import jax
import jax.numpy as jnp
from jax import lax
from jax.sharding import PartitionSpec as P

STAT_DECAY = 0.95
ADAM_DECAY = 0.95
LEARN_RATE = 0.1
NORM_EPS = 1e-06


def slot_onehot(owner_ids, capacity, slot_count):
    position = jnp.arange(owner_ids.shape[0], dtype=jnp.int32)
    same_owner = owner_ids[:, None] == owner_ids[None, :]
    earlier = position[None, :] < position[:, None]
    slot_rank = jnp.sum((same_owner & earlier).astype(jnp.int32), axis=1)
    target = owner_ids * capacity + slot_rank
    return (target[:, None] == jnp.arange(slot_count, dtype=jnp.int32)[None, :]).astype(
        jnp.bfloat16
    )


def shampoo(gradient, weights, left, right, left_root, right_root, second):
    high = lax.Precision.HIGHEST
    new_left = STAT_DECAY * left + (1.0 - STAT_DECAY) * jnp.einsum(
        "...ij,...kj->...ik", gradient, gradient, precision=high
    )
    new_right = STAT_DECAY * right + (1.0 - STAT_DECAY) * jnp.einsum(
        "...ji,...jk->...ik", gradient, gradient, precision=high
    )
    shaped = jnp.einsum("...ij,...jk->...ik", left_root, gradient, precision=high)
    shaped = jnp.einsum("...ij,...jk->...ik", shaped, right_root, precision=high)
    new_second = ADAM_DECAY * second + (1.0 - ADAM_DECAY) * gradient * gradient
    adam_step = gradient / jnp.sqrt(new_second)
    adam_norm = jnp.sqrt(jnp.sum(adam_step * adam_step, axis=(-2, -1), keepdims=True))
    shaped_norm = jnp.sqrt(jnp.sum(shaped * shaped, axis=(-2, -1), keepdims=True))
    graft_scale = adam_norm / (shaped_norm + NORM_EPS)
    new_weights = weights - LEARN_RATE * graft_scale * shaped
    return (new_weights, new_left, new_right, new_second)


def on_device(value_grads, key_grads, owners, weights, left, right, left_root, right_root, second):
    dp_count = lax.axis_size("dp")
    capacity = weights.shape[2]
    slot_count = dp_count * capacity
    value_count = value_grads.shape[1]
    side = value_grads.shape[2]
    key_part = lax.psum_scatter(
        key_grads.astype(jnp.float32).astype(jnp.bfloat16), "mp", scatter_dimension=2, tiled=True
    ).astype(jnp.float32)
    key_rows = key_part[0, 0].astype(jnp.bfloat16)
    one_hot = slot_onehot(owners[:, 0], capacity, slot_count)
    blocks = jnp.concatenate([value_grads[0], key_rows], axis=0)
    placed = jnp.einsum("bj,bxy->jxy", one_hot, blocks, preferred_element_type=jnp.float32)
    outgoing = placed.astype(jnp.bfloat16).reshape(dp_count, capacity, side, side)
    incoming = lax.all_to_all(outgoing, "dp", split_axis=0, concat_axis=0, tiled=True)
    gradient = jnp.sum(incoming, axis=0, dtype=jnp.float32)
    new_weights, new_left, new_right, new_second = shampoo(
        gradient,
        weights[0, 0],
        left[0, 0],
        right[0, 0],
        left_root[0, 0],
        right_root[0, 0],
        second[0, 0],
    )
    rounded = new_weights.astype(jnp.bfloat16)
    everyone = lax.all_gather(rounded, "dp", axis=0, tiled=True)
    picked = jnp.einsum(
        "bj,jxy->bxy", one_hot, everyone, preferred_element_type=jnp.float32
    ).astype(jnp.bfloat16)
    return (
        new_weights[None, None],
        new_left[None, None],
        new_right[None, None],
        new_second[None, None],
        picked[:value_count],
        picked[value_count:],
    )


def solution(mesh):
    return jax.shard_map(
        on_device,
        mesh=mesh,
        in_specs=(
            P("dp", "mp", None, None),
            P("dp", "mp", None, None, None),
            P("mp", None),
            P("dp", "mp", None, None, None),
            P("dp", "mp", None, None, None),
            P("dp", "mp", None, None, None),
            P("dp", "mp", None, None, None),
            P("dp", "mp", None, None, None),
            P("dp", "mp", None, None, None),
        ),
        out_specs=(
            P("dp", "mp", None, None, None),
            P("dp", "mp", None, None, None),
            P("dp", "mp", None, None, None),
            P("dp", "mp", None, None, None),
            P("mp", None, None),
            P("mp", None, None),
        ),
        check_vma=False,
    )
```

profile of v0, /device:TPU:0, one launch (start us, length us, event | category | flops | bytes accessed | tf_op | source)
XLA Modules:
  0.0 123.6 jit_solution(12774246260677728813)
XLA Ops:
  7.2 0.0 copy-start
  7.2 0.0 copy-start.2
  7.2 0.0 reduce-scatter.4.cloned.1.call-start
  7.2 0.0 copy-start.7
  7.2 2.2 %copy.86 = bf16[2,8,128,128]{3,1,2,0:T(8,128)(2,1)} copy(bf16[2,8,128,128]{3,2,1,0:T(8,128)(2,1)} %bitcast.74) | data formatting | bytes 1048576
  9.5 0.0 reduce-scatter.4.cloned.1.call-update
  9.5 0.0 all-gather.2.cloned.1.call-start
  9.5 0.0 copy-done.2
  9.6 0.3 copy.87
  9.8 0.0 copy-done.7
  9.8 0.2 convert_reduce_fusion.1
  10.0 10.9 %reduce-scatter.4.cloned.1.call-done = bf16[8,16384]{1,0:T(8,128)(2,1)} async-done(((bf16[16,16384]{1,0:T(8,128)(2,1)}), bf16[8,16384]{1,0:T(8,128)(2,1)}) %reduce-scatter.4.cloned.1.call-update) | async-done | bytes 262160
  20.9 1.0 copy.88
  21.9 0.2 copy.89
  22.1 0.6 convolution_convert_fusion
  22.7 1.0 copy.55
  23.6 33.3 %all_to_all.5 = bf16[16,2,128,128]{3,1,2,0:T(2,128)(2,1)S(1)} all-to-all(bf16[16,2,128,128]{3,1,2,0:T(2,128)(2,1)S(1)} %copy.55), channel_id=1, replica_groups=mesh['dp'=16,'mp'=2] {'dp'}, dimensions={0} | all-to-all | bytes 2097152 | tf_op jit(solution)/shard_map/all_to_all | solution.py:56
  56.9 0.1 convert_reduce_fusion
  57.0 0.8 copy-done.3
  57.8 0.3 fusion.16
  58.1 0.1 fusion.12
  58.2 0.4 multiply_reduce_fusion
  58.6 0.8 fusion.18
  59.4 0.0 all-gather.2.cloned.1.call-update
  59.4 1.0 fusion.1
  60.5 1.0 fusion.3
  61.5 0.7 fusion.13
  62.2 50.9 %all-gather.2.cloned.1.call-done = bf16[32,128,128]{2,1,0:T(8,128)(2,1)} async-done(((bf16[2,128,128]{2,1,0:T(8,128)(2,1)}), bf16[32,128,128]{2,1,0:T(8,128)(2,1)}) %all-gather.2.cloned.1.call-update) | async-done | bytes 1048592 | tf_op jit(solution)/shard_map/all_gather | solution.py:68
  113.1 2.0 %convolution_convert_fusion.1 = bf16[20,128,128]{2,0,1:T(8,128)(2,1)S(1)} fusion(bf16[32,128,128]{2,1,0:T(8,128)(2,1)} %all-gather.2.cloned.1.call-done, s32[20]{0:T(128)S(1)} %fusion.26), kind=kOutput, calls=%fused_computation.2 | convolution fusion | flops 21299840 | bytes 1704016 | tf_op jit(solution)/shard_map/bj,jxy->bxy/dot_general | solution.py:69
  115.1 0.1 slice.9
  115.2 0.8 copy.69
  116.0 0.7 copy.70
  (13 shorter events, 0.1 us)
Async XLA Ops:
  7.2 51.0 %copy-start = (f32[1,1,2,128,128]{4,3,2,1,0:T(8,128)S(1)}, f32[1,1,2,128,128]{4,3,2,1,0:T(8,128)}, u32[]{:S(2)}) copy-start(f32[1,1,2,128,128]{4,3,2,1,0:T(8,128)} %param.16) | copy-start | bytes 393220
  7.2 2.4 %copy-start.2 = (bf16[1,12,128,128]{3,2,1,0:T(8,128)(2,1)S(1)}, bf16[1,12,128,128]{3,2,1,0:T(8,128)(2,1)}, u32[]{:S(2)}) copy-start(bf16[1,12,128,128]{3,2,1,0:T(8,128)(2,1)} %param.9) | copy-start | bytes 1179652
  7.2 13.7 %reduce-scatter.4.cloned.1.call-start = ((), (), s32[]{:S(2)}) async-start(), calls=%async_computation.3 | async-start | bytes 786432
  7.2 2.6 %copy-start.7 = (s32[20,1]{0,1:T(1,128)S(1)}, s32[20,1]{0,1:T(1,128)}, u32[]{:S(2)}) copy-start(s32[20,1]{0,1:T(1,128)} %param.11) | copy-start | bytes 244
  9.5 103.6 %all-gather.2.cloned.1.call-start = ((), (), s32[]{:S(2)}) async-start(), calls=%async_computation.2 | async-start | bytes 1114112 | tf_op jit(solution)/shard_map/all_gather | solution.py:68
  56.9 0.9 copy-start.3
  56.9 1.2 copy-start.1
  56.9 1.7 %copy-start.4 = (f32[1,1,2,128,128]{4,3,2,1,0:T(8,128)S(1)}, f32[1,1,2,128,128]{4,3,2,1,0:T(8,128)}, u32[]{:S(2)}) copy-start(f32[1,1,2,128,128]{4,3,2,1,0:T(8,128)} %param.12) | copy-start | bytes 393220
  57.8 1.6 %copy-start.5 = (f32[1,1,2,128,128]{4,3,2,1,0:T(8,128)S(1)}, f32[1,1,2,128,128]{4,3,2,1,0:T(8,128)}, u32[]{:S(2)}) copy-start(f32[1,1,2,128,128]{4,3,2,1,0:T(8,128)} %param.14) | copy-start | bytes 393220
  57.8 2.7 %copy-start.6 = (f32[1,1,2,128,128]{4,3,2,1,0:T(8,128)S(1)}, f32[1,1,2,128,128]{4,3,2,1,0:T(8,128)}, u32[]{:S(2)}) copy-start(f32[1,1,2,128,128]{4,3,2,1,0:T(8,128)} %param.13) | copy-start | bytes 393220
Sparse Core Ops, SparseCore 0:
  10.2 10.6 reduce-scatter.3
  59.5 53.5 all-gather.1
where the time goes:
time: 124 us
  waiting for transfers between devices  61.8 us (50%)
  blocking collectives  33.3 us (27%)
  between operations  14.2 us (11%)
  local copies, waits for them, and re-layouts  7.18 us (6%)
  matrix products  5.23 us (4%)
  other arithmetic  1.86 us (2%)
    all_gather x1, waiting for transfers between devices, on_device(): everyone = lax.all_gather(rounded, 'dp', axis=0, tiled=True)  50.9 us
    all_to_all x1, blocking collectives, on_device(): lax.all_to_all(outgoing, 'dp', split_axis=0, concat_axis=0, tiled=True)  33.3 us
    unnamed x3, waiting for transfers between devices  10.9 us
    unnamed x22, local copies, waits for them, and re-layouts  6.1 us
  transfers between devices with their start and end apart: 2, of which 2 were waited for; matrix products, arithmetic and copies ran while one was open for 3% of the time, Pallas kernels for 0%

commit v1 on v0

--- a/solution.py
+++ b/solution.py
@@ -7,6 +7,18 @@
 ADAM_DECAY = 0.95
 LEARN_RATE = 0.1
 NORM_EPS = 1e-06
+
+
+def collect(array, axis, dim):
+    ways, here, hop = (lax.axis_size(axis), lax.axis_index(axis), array.shape[dim])
+    line, have = (array, 1)
+    while have < ways:
+        line = jnp.concatenate(
+            [line, lax.ppermute(line, axis, [(d, (d - have) % ways) for d in range(ways)])],
+            axis=dim,
+        )
+        have = 2 * have
+    return jnp.roll(line, here * hop, axis=dim)
 
 
 def slot_onehot(owner_ids, capacity, slot_count):
@@ -65,7 +77,7 @@
         second[0, 0],
     )
     rounded = new_weights.astype(jnp.bfloat16)
-    everyone = lax.all_gather(rounded, "dp", axis=0, tiled=True)
+    everyone = collect(rounded, "dp", 0)
     picked = jnp.einsum(
         "bj,jxy->bxy", one_hot, everyone, preferred_element_type=jnp.float32
     ).astype(jnp.bfloat16)

time: 124 us -> 110 us (0.89)
  the two profiles are of different devices: /device:TPU:0 before, /device:TPU:31 now
where the time goes in v1:
time: 110 us
  waiting for transfers between devices  51.2 us (47%)
  blocking collectives  29.5 us (27%)
  between operations  14.3 us (13%)
  local copies, waits for them, and re-layouts  7.72 us (7%)
  matrix products  4.02 us (4%)
  other arithmetic  2.01 us (2%)
  starting transfers between devices  1.37 us (1%)
    ppermute x4, waiting for transfers between devices, collect(): lax.ppermute(line, axis, [(d, (d - have) % ways) for d in range(ways)])  42.2 us
    all_to_all x1, blocking collectives, on_device(): lax.all_to_all(outgoing, 'dp', split_axis=0, concat_axis=0, tiled=True)  29.5 us
    unnamed x2, waiting for transfers between devices  8.94 us
    unnamed x28, local copies, waits for them, and re-layouts  6.46 us
  transfers between devices with their start and end apart: 5, of which 5 were waited for; matrix products, arithmetic and copies ran while one was open for 5% of the time, Pallas kernels for 0%

profile of v1, /device:TPU:31, one launch (start us, length us, event | category | flops | bytes accessed | tf_op | source)
XLA Modules:
  0.0 110.0 jit_solution(12268200680307725274)
XLA Ops:
  7.2 2.2 %copy.86 = bf16[2,8,128,128]{3,1,2,0:T(8,128)(2,1)} copy(bf16[2,8,128,128]{3,2,1,0:T(8,128)(2,1)} %bitcast.75) | data formatting | bytes 1048576
  9.4 1.3 %copy.87 = bf16[1,12,128,128]{3,1,2,0:T(8,128)(2,1)S(1)} copy(bf16[1,12,128,128]{3,2,1,0:T(8,128)(2,1)} %param.9) | data formatting | bytes 786432 | tf_op args[0]
  10.7 0.2 convert_reduce_fusion.1
  10.9 8.9 %reduce-scatter.4.cloned.1.call-done = bf16[8,16384]{1,0:T(8,128)(2,1)} async-done(((bf16[16,16384]{1,0:T(8,128)(2,1)}), bf16[8,16384]{1,0:T(8,128)(2,1)}) %reduce-scatter.4.cloned.1.call-update) | async-done | bytes 262160
  19.8 1.0 copy.88
  20.8 0.2 copy.89
  21.0 0.6 convolution_convert_fusion
  21.6 1.0 copy.55
  22.6 29.5 %all_to_all.5 = bf16[16,2,128,128]{3,1,2,0:T(2,128)(2,1)S(1)} all-to-all(bf16[16,2,128,128]{3,1,2,0:T(2,128)(2,1)S(1)} %copy.55), channel_id=1, replica_groups=mesh['dp'=16,'mp'=2] {'dp'}, dimensions={0} | all-to-all | bytes 2097152 | tf_op jit(solution)/shard_map/all_to_all | solution.py:68
  52.0 0.1 convert_reduce_fusion
  52.1 0.3 fusion.16
  52.4 0.1 fusion.12
  52.6 0.4 multiply_reduce_fusion
  53.0 0.1 constant_dynamic-update-slice_fusion.9
  53.1 1.1 %collective-permute-start = (bf16[2,128,128]{2,1,0:T(8,128)(2,1)S(1)}, bf16[2,128,128]{2,1,0:T(8,128)(2,1)S(1)}, u32[]{:S(2)}, u32[]{:S(2)}) collective-permute-start(bf16[2,128,128]{2,1,0:T(8,128)(2,1)S(1)} %get-tuple-element.31), channel_id=1, source_target_pairs={{0,30},{2,0},{4,2},{6,4},{8,6},{10,8},{12,10},{14,12},{16,14},{18,... | collective-permute-start | bytes 196616 | tf_op jit(solution)/shard_map/ppermute | solution.py:17
  54.2 5.6 %collective-permute-done = bf16[2,128,128]{2,1,0:T(8,128)(2,1)S(1)} collective-permute-done((bf16[2,128,128]{2,1,0:T(8,128)(2,1)S(1)}, bf16[2,128,128]{2,1,0:T(8,128)(2,1)S(1)}, u32[]{:S(2)}, u32[]{:S(2)}) %collective-permute-start) | collective-permute-done | bytes 65568 | tf_op jit(solution)/shard_map/ppermute | solution.py:17
  59.8 0.1 collective-permute-start.1
  59.9 6.5 %collective-permute-done.1 = bf16[4,128,128]{2,1,0:T(8,128)(2,1)S(1)} collective-permute-done((bf16[4,128,128]{2,1,0:T(8,128)(2,1)S(1)}, bf16[4,128,128]{2,1,0:T(8,128)(2,1)S(1)}, u32[]{:S(2)}, u32[]{:S(2)}) %collective-permute-start.1) | collective-permute-done | bytes 131104 | tf_op jit(solution)/shard_map/ppermute | solution.py:17
  66.5 0.7 fusion.13
  67.2 0.7 fusion.19
  67.9 5.6 %collective-permute-done.2 = bf16[8,128,128]{2,1,0:T(8,128)(2,1)S(1)} collective-permute-done((bf16[8,128,128]{2,1,0:T(8,128)(2,1)S(1)}, bf16[8,128,128]{2,1,0:T(8,128)(2,1)S(1)}, u32[]{:S(2)}, u32[]{:S(2)}) %collective-permute-start.2) | collective-permute-done | bytes 262176 | tf_op jit(solution)/shard_map/ppermute | solution.py:17
  73.6 0.1 collective-permute-start.3
  73.7 1.0 fusion.1
  74.7 1.0 fusion.3
  75.8 24.5 %collective-permute-done.3 = bf16[16,128,128]{2,1,0:T(8,128)(2,1)S(1)} collective-permute-done((bf16[16,128,128]{2,1,0:T(8,128)(2,1)S(1)}, bf16[16,128,128]{2,1,0:T(8,128)(2,1)S(1)}, u32[]{:S(2)}, u32[]{:S(2)}) %collective-permute-start.3) | collective-permute-done | bytes 524320 | tf_op jit(solution)/shard_map/ppermute | solution.py:17
  100.4 0.1 constant_dynamic-update-slice_fusion.5
  100.5 0.1 constant_dynamic-update-slice_fusion
  100.6 0.1 constant_dynamic-slice_fusion
  100.7 0.7 convolution_convert_fusion.1
  101.5 0.1 slice.9
  101.6 0.8 copy.69
  102.5 0.7 copy.70
  (30 shorter events, 0.5 us)
Async XLA Ops:
  7.2 45.4 %copy-start = (f32[1,1,2,128,128]{4,3,2,1,0:T(8,128)S(1)}, f32[1,1,2,128,128]{4,3,2,1,0:T(8,128)}, u32[]{:S(2)}) copy-start(f32[1,1,2,128,128]{4,3,2,1,0:T(8,128)} %param.16) | copy-start | bytes 393220
  7.2 3.5 %copy-start.6 = (s32[20,1]{0,1:T(1,128)S(1)}, s32[20,1]{0,1:T(1,128)}, u32[]{:S(2)}) copy-start(s32[20,1]{0,1:T(1,128)} %param.11) | copy-start | bytes 244
  7.2 12.6 %reduce-scatter.4.cloned.1.call-start = ((), (), s32[]{:S(2)}) async-start(), calls=%async_computation.2 | async-start | bytes 786432
  22.5 29.6 %copy-start.3 = (f32[1,1,2,128,128]{4,3,2,1,0:T(8,128)S(1)}, f32[1,1,2,128,128]{4,3,2,1,0:T(8,128)}, u32[]{:S(2)}) copy-start(f32[1,1,2,128,128]{4,3,2,1,0:T(8,128)} %param.15) | copy-start | bytes 393220
  22.5 29.9 %copy-start.1 = (f32[1,1,2,128,128]{4,3,2,1,0:T(8,128)S(1)}, f32[1,1,2,128,128]{4,3,2,1,0:T(8,128)}, u32[]{:S(2)}) copy-start(f32[1,1,2,128,128]{4,3,2,1,0:T(8,128)} %param.17) | copy-start | bytes 393220
  22.6 30.4 %copy-start.2 = (f32[1,1,2,128,128]{4,3,2,1,0:T(8,128)S(1)}, f32[1,1,2,128,128]{4,3,2,1,0:T(8,128)}, u32[]{:S(2)}) copy-start(f32[1,1,2,128,128]{4,3,2,1,0:T(8,128)} %param.12) | copy-start | bytes 393220
  52.1 21.5 %copy-start.4 = (f32[1,1,2,128,128]{4,3,2,1,0:T(8,128)S(1)}, f32[1,1,2,128,128]{4,3,2,1,0:T(8,128)}, u32[]{:S(2)}) copy-start(f32[1,1,2,128,128]{4,3,2,1,0:T(8,128)} %param.14) | copy-start | bytes 393220
  52.4 22.3 %copy-start.5 = (f32[1,1,2,128,128]{4,3,2,1,0:T(8,128)S(1)}, f32[1,1,2,128,128]{4,3,2,1,0:T(8,128)}, u32[]{:S(2)}) copy-start(f32[1,1,2,128,128]{4,3,2,1,0:T(8,128)} %param.13) | copy-start | bytes 393220
  53.1 6.8 %collective-permute-start = (bf16[2,128,128]{2,1,0:T(8,128)(2,1)S(1)}, bf16[2,128,128]{2,1,0:T(8,128)(2,1)S(1)}, u32[]{:S(2)}, u32[]{:S(2)}) collective-permute-start(bf16[2,128,128]{2,1,0:T(8,128)(2,1)S(1)} %get-tuple-element.31), channel_id=1, source_target_pairs={{0,30},{2,0},{4,2},{6,4},{8,6},{10,8},{12,10},{14,12},{16,14},{18,... | collective-permute-start | bytes 196616 | tf_op jit(solution)/shard_map/ppermute | solution.py:17
  59.8 6.6 %collective-permute-start.1 = (bf16[4,128,128]{2,1,0:T(8,128)(2,1)S(1)}, bf16[4,128,128]{2,1,0:T(8,128)(2,1)S(1)}, u32[]{:S(2)}, u32[]{:S(2)}) collective-permute-start(bf16[4,128,128]{2,1,0:T(8,128)(2,1)S(1)} %pad_maximum_fusion.2), channel_id=1, source_target_pairs={{0,28},{2,30},{4,0},{6,2},{8,4},{10,6},{12,8},{14,10},{16,12},{18,... | collective-permute-start | bytes 393224 | tf_op jit(solution)/shard_map/ppermute | solution.py:17
  66.4 7.1 %collective-permute-start.2 = (bf16[8,128,128]{2,1,0:T(8,128)(2,1)S(1)}, bf16[8,128,128]{2,1,0:T(8,128)(2,1)S(1)}, u32[]{:S(2)}, u32[]{:S(2)}) collective-permute-start(bf16[8,128,128]{2,1,0:T(8,128)(2,1)S(1)} %pad_maximum_fusion.1), channel_id=1, source_target_pairs={{0,24},{2,26},{4,28},{6,30},{8,0},{10,2},{12,4},{14,6},{16,8},{18,... | collective-permute-start | bytes 786440 | tf_op jit(solution)/shard_map/ppermute | solution.py:17
  73.6 26.8 %collective-permute-start.3 = (bf16[16,128,128]{2,1,0:T(8,128)(2,1)S(1)}, bf16[16,128,128]{2,1,0:T(8,128)(2,1)S(1)}, u32[]{:S(2)}, u32[]{:S(2)}) collective-permute-start(bf16[16,128,128]{2,1,0:T(8,128)(2,1)S(1)} %pad_maximum_fusion), channel_id=1, source_target_pairs={{0,16},{2,18},{4,20},{6,22},{8,24},{10,26},{12,28},{14,30},{16,0},... | collective-permute-start | bytes 1572872 | tf_op jit(solution)/shard_map/ppermute | solution.py:17
Sparse Core Ops, SparseCore 0:
  10.2 9.5 reduce-scatter.3
